TPU v7x, 32 devices: a whole 2x2x4 slice. The times are simulated.
32 devices in a mesh: ka: 16 (over z, y, core), aux: 2 (over x).
Axes of the slice: x: 2, y: 2, z: 4, core: 2. Of those that a mesh axis runs over, the one named last changes fastest.
Arguments:
- coefficients: bfloat16 [16, 4096, 128], P('ka'), may hold values from -2.09375 to 2.09375
- triple: bfloat16 [64, 2, 64, 768], P('aux'), may hold values from -0.5 to 0.5
- neighbors: int32 [64, 2], P('aux'), may hold values from 0 to 63
- w_screened: bfloat16 [16, 768, 1536], P('ka', 'aux'), as said below
- partner: int32 [2, 16], replicated, may hold values from 0 to 15, each once within a row
- q_ids: int32 [2], replicated, may hold values from 0 to 15
Outputs:
- sigma: float32 [16, 64, 128], P('ka', 'aux')
Inputs may be any that keep to these rules, and one draw needn't show every extreme that they name: Each stored w_screened is Hermitian: its real block is symmetric and its imaginary block antisymmetric.
All inputs are finite; a program needn't handle non-finite values.
Results may differ from a plain program's by a relative error of at most 0.0085.
Values may be sent and summed in bfloat16 or wider, within the bound.
A program may use at most 128 MiB of HBM per device.

v0:
```python
import math
import jax
import jax.numpy as jnp
from jax import lax
from jax.sharding import PartitionSpec as P

CELL_ATOMS = 64
ORBITALS_PER_ATOM = 64
AUX_ATOM = 12
OCCUPIED_BANDS = 16
TRANSFERS = 2
NAUX = 768


def from_root(block, axis, source):
    block = jnp.where(lax.axis_index(axis) == source, block, jnp.zeros_like(block))
    return lax.psum(block, axis)


def from_partner(value, axis, distance):
    mask = 2**distance
    pairs = [(source, source ^ mask) for source in range(lax.axis_size(axis))]
    return lax.ppermute(value, axis, pairs)


def rotated_parts(values, band_count):
    return jnp.concatenate([-values[..., band_count:], values[..., :band_count]], axis=-1)


def apply_block(weights, start, values, band_count):
    kpoints, rows, occupied, doubled = values.shape
    real_cols = lax.dynamic_slice_in_dim(weights, start, rows, 1)
    imag_cols = lax.dynamic_slice_in_dim(weights, NAUX + start, rows, 1)
    flat = values.reshape(kpoints, rows, occupied * doubled)
    turned = rotated_parts(values, band_count).reshape(kpoints, rows, occupied * doubled)
    result = jnp.einsum("ab,kbx->kax", real_cols, flat, preferred_element_type=jnp.float32)
    result = result + jnp.einsum(
        "ab,kbx->kax", imag_cols, turned, preferred_element_type=jnp.float32
    )
    return result.reshape(kpoints, weights.shape[0], occupied, doubled)


def pair_blocks(left_values, right_values):
    kpoints = left_values.shape[0]
    doubled = left_values.shape[-1]
    left_flat = left_values.reshape(kpoints, -1, doubled)
    right_flat = right_values.reshape(kpoints, -1, doubled)
    return jnp.einsum("kxm,kxn->kmn", left_flat, right_flat, preferred_element_type=jnp.float32)


def sigma_parts(blocks, band_count):
    sigma_real = blocks[:, :band_count, :band_count] + blocks[:, band_count:, band_count:]
    sigma_imag = blocks[:, :band_count, band_count:] - blocks[:, band_count:, :band_count]
    return (sigma_real, sigma_imag)


def local(coefficients, triple, neighbors, w_screened, partner, q_ids):
    kpoints, orbitals, doubled = coefficients.shape
    band_count = doubled // 2
    local_atoms = triple.shape[0]
    local_aux = local_atoms * AUX_ATOM
    half_index = lax.axis_index("aux")
    prefactor = -1.0 / math.sqrt(TRANSFERS * NAUX * OCCUPIED_BANDS)
    screens = [
        from_root(w_screened[0], "ka", q_ids[momentum_transfer])
        for momentum_transfer in range(TRANSFERS)
    ]
    far_cols = jnp.concatenate(
        [
            coefficients[:, :, :OCCUPIED_BANDS],
            coefficients[:, :, band_count : band_count + OCCUPIED_BANDS],
        ],
        axis=2,
    )
    packed = far_cols.reshape(kpoints, orbitals * 2 * OCCUPIED_BANDS // 128, 128)
    spread = lax.all_to_all(packed, "ka", split_axis=1, concat_axis=0, tiled=True)
    permuted = jnp.take(spread, partner, axis=0)
    arrived = jnp.stack(
        [
            lax.all_to_all(
                permuted[momentum_transfer], "ka", split_axis=0, concat_axis=1, tiled=True
            )
            for momentum_transfer in range(TRANSFERS)
        ]
    )
    distant_coefficients = arrived.reshape(
        TRANSFERS, kpoints, CELL_ATOMS, ORBITALS_PER_ATOM, 2 * OCCUPIED_BANDS
    )
    own_rows = lax.dynamic_slice_in_dim(
        coefficients,
        half_index * local_atoms * ORBITALS_PER_ATOM,
        local_atoms * ORBITALS_PER_ATOM,
        1,
    )
    home_coefficients = own_rows.reshape(kpoints, local_atoms, ORBITALS_PER_ATOM, doubled)
    neighbour_coef = jnp.take(distant_coefficients, neighbors, axis=2)
    pair_half = jnp.einsum(
        "tkcjoy,cjox->tkcyx", neighbour_coef, triple, preferred_element_type=jnp.float32
    ).astype(jnp.bfloat16)
    pair_half = pair_half.reshape(
        TRANSFERS, kpoints, local_atoms, 2 * OCCUPIED_BANDS, AUX_ATOM, ORBITALS_PER_ATOM
    )
    combos = jnp.einsum(
        "kcix,tkcyai->tkcayx", home_coefficients, pair_half, preferred_element_type=jnp.float32
    )
    real_part = (
        combos[..., :OCCUPIED_BANDS, :band_count] + combos[..., OCCUPIED_BANDS:, band_count:]
    )
    imag_part = (
        combos[..., OCCUPIED_BANDS:, :band_count] - combos[..., :OCCUPIED_BANDS, band_count:]
    )
    products = jnp.concatenate([real_part, imag_part], axis=-1).astype(jnp.bfloat16)
    products = products.reshape(TRANSFERS, kpoints, local_aux, OCCUPIED_BANDS, doubled)
    pairs = products.reshape(TRANSFERS // 2, 2, kpoints, local_aux, OCCUPIED_BANDS, doubled)
    screen_pairs = jnp.stack(screens).reshape(TRANSFERS // 2, 2, local_aux, 2 * NAUX)
    outgoing = lax.dynamic_index_in_dim(pairs, 1 - half_index, 1, keepdims=False)
    incoming = from_partner(outgoing, "aux", 0)
    own_start = half_index * local_aux
    other_start = (1 - half_index) * local_aux
    full_weights = lax.dynamic_index_in_dim(screen_pairs[0], half_index, 0, keepdims=False)
    part_weights = lax.dynamic_index_in_dim(screen_pairs[0], 1 - half_index, 0, keepdims=False)
    full_values = lax.dynamic_index_in_dim(pairs[0], half_index, 0, keepdims=False)
    part_values = lax.dynamic_index_in_dim(pairs[0], 1 - half_index, 0, keepdims=False)
    cross = apply_block(full_weights, other_start, incoming[0], band_count)
    full_screened = (apply_block(full_weights, own_start, full_values, band_count) + cross).astype(
        jnp.bfloat16
    )
    part_screened = apply_block(part_weights, own_start, part_values, band_count).astype(
        jnp.bfloat16
    )
    cross_screened = cross.astype(jnp.bfloat16)
    diagonal = pair_blocks(full_values, full_screened) + pair_blocks(part_values, part_screened)
    diag_real, diag_imag = sigma_parts(diagonal, band_count)
    cross_real, cross_imag = sigma_parts(pair_blocks(full_values, cross_screened), band_count)
    total_real = diag_real + jnp.transpose(cross_real, (0, 2, 1))
    total_imag = diag_imag - jnp.transpose(cross_imag, (0, 2, 1))
    local_sigma = jnp.concatenate([total_real, total_imag], axis=-1)
    local_sigma = prefactor * local_sigma
    return lax.psum_scatter(
        local_sigma.astype(jnp.bfloat16), "aux", scatter_dimension=1, tiled=True
    ).astype(jnp.float32)


def solution(mesh):
    in_specs = (
        P("ka", None, None),
        P("aux", None, None, None),
        P("aux", None),
        P("ka", "aux", None),
        P(),
        P(),
    )
    out_specs = P("ka", "aux", None)
    return jax.shard_map(local, mesh=mesh, in_specs=in_specs, out_specs=out_specs, check_vma=False)
```

profile of v0, /device:TPU:0, one launch (start us, length us, event | category | flops | bytes accessed | tf_op | source)
XLA Modules:
  0.0 210.7 jit_solution(5651449956877544662)
XLA Ops:
  6.5 2.1 fusion.62
  10.9 2.2 %reduce = bf16[1024,128]{1,0:T(8,128)(2,1)S(1)} reduce(bf16[1024,1,128]{2,1,0:T(2,128)(2,1)S(1)} %bitcast.159, bf16[]{:T(256)} %broadcast.52), dimensions={1}, to_apply=%bitcast.134.reduce_sub_computation | reduce | bytes 524290
  13.1 0.8 reshape.297
  13.9 7.4 %all-to-all-start = ((bf16[16,2,4096]{2,1,0:T(2,128)(2,1)}), bf16[16,2,4096]{2,1,0:T(2,128)(2,1)S(1)}, u32[]{:S(2)}, u32[]{:S(2)}) async-start(bf16[16,2,4096]{2,1,0:T(2,128)(2,1)} %reshape.297), calls=%async_computation | async-start | bytes 524288 | tf_op jit(solution)/shard_map/all_to_all | solution.py:76
  23.3 8.0 %all-to-all-done = bf16[16,2,4096]{2,1,0:T(2,128)(2,1)S(1)} async-done(((bf16[16,2,4096]{2,1,0:T(2,128)(2,1)}), bf16[16,2,4096]{2,1,0:T(2,128)(2,1)S(1)}, u32[]{:S(2)}, u32[]{:S(2)}) %all-to-all-start) | async-done | bytes 262176 | tf_op jit(solution)/shard_map/all_to_all | solution.py:76
  32.4 0.8 slice_bitcast_fusion.1
  33.3 3.5 %all-to-all-start.1 = ((bf16[16,64,128]{2,1,0:T(8,128)(2,1)}), bf16[16,64,128]{2,1,0:T(8,128)(2,1)S(1)}, u32[]{:S(2)}, u32[]{:S(2)}) async-start(bf16[16,64,128]{2,1,0:T(8,128)(2,1)} %get-tuple-element.21), calls=%async_computation.1 | async-start | bytes 524288 | tf_op jit(solution)/shard_map/all_to_all | solution.py:80
  36.9 1.6 broadcast_select_fusion
  39.3 7.4 %all-to-all-done.1 = bf16[16,64,128]{2,1,0:T(8,128)(2,1)S(1)} async-done(((bf16[16,64,128]{2,1,0:T(8,128)(2,1)}), bf16[16,64,128]{2,1,0:T(8,128)(2,1)S(1)}, u32[]{:S(2)}, u32[]{:S(2)}) %all-to-all-start.1) | async-done | bytes 262176 | tf_op jit(solution)/shard_map/all_to_all | solution.py:80
  46.8 3.5 %all-to-all-start.2 = ((bf16[16,64,128]{2,1,0:T(8,128)(2,1)}), bf16[16,64,128]{2,1,0:T(8,128)(2,1)S(1)}, u32[]{:S(2)}, u32[]{:S(2)}) async-start(bf16[16,64,128]{2,1,0:T(8,128)(2,1)} %get-tuple-element.22), calls=%async_computation.2 | async-start | bytes 524288 | tf_op jit(solution)/shard_map/all_to_all | solution.py:80
  50.7 0.8 constant_dynamic-slice_fusion
  52.0 11.2 %all-to-all-done.2 = bf16[16,64,128]{2,1,0:T(8,128)(2,1)S(1)} async-done(((bf16[16,64,128]{2,1,0:T(8,128)(2,1)}), bf16[16,64,128]{2,1,0:T(8,128)(2,1)S(1)}, u32[]{:S(2)}, u32[]{:S(2)}) %all-to-all-start.2) | async-done | bytes 262176 | tf_op jit(solution)/shard_map/all_to_all | solution.py:80
  63.1 1.4 stack.19
  64.5 1.7 maximum_bitcast_fusion
  66.2 2.1 %gather_fusion.1 = bf16[64,2,64,32]{3,2,1,0:T(8,128)(2,1)} fusion(bf16[2,64,64,32]{3,2,1,0:T(8,128)(2,1)S(1)} %maximum_bitcast_fusion, s32[1024]{0:T(1024)S(1)} %pad_clamp_fusion), kind=kCustom, calls=%fused_computation.1 | custom fusion | bytes 1048832 | tf_op jit(solution)/shard_map/jit(_take)/gather | solution.py:96
  68.4 2.8 %copy.46 = bf16[64,2,64,32]{2,3,1,0:T(8,128)(2,1)} copy(bf16[64,2,64,32]{3,2,1,0:T(8,128)(2,1)} %gather_fusion.1) | data formatting | bytes 1048576 | tf_op jit(solution)/shard_map/jit(_take)/gather | solution.py:96
  71.1 4.9 %fusion.9 = bf16[2,1,32,32,768]{4,3,0,2,1:T(8,128)(2,1)S(1)} fusion(bf16[32,2,64,768]{3,2,1,0:T(8,128)(2,1)} %param.7, bf16[32,2,2,64,32]{3,4,2,1,0:T(8,128)(2,1)} %bitcast.155, pred[32,2]{1,0:T(8,128)(4,1)S(1)} %copy.40), kind=kOutput, calls=%fused_computation.12 | convolution fusion | flops 404488192 | bytes 9961536 | tf_op jit(solution)/shard_map/tkcjoy,cjox->tkcyx/dot_general | solution.py:97
  76.0 7.2 %reshape.296 = bf16[2,32,32,12,64]{4,3,2,0,1:T(8,128)(2,1)} reshape(bf16[2,1,32,32,768]{4,3,0,2,1:T(8,128)(2,1)S(1)} %fusion.9) | data formatting | bytes 6291456 | tf_op jit(solution)/shard_map/reshape.12
  83.2 5.1 %fusion.6 = f32[2,1,32,12,32,128]{5,4,3,0,2,1:T(8,128)S(1)} fusion(bf16[32,64,128,1,1]{2,1,4,3,0:T(8,128)(2,1)} %bitcast.160, bf16[2,32,32,12,64]{4,3,2,0,1:T(8,128)(2,1)} %reshape.296), kind=kOutput, calls=%fused_computation.11 | convolution fusion | flops 402653184 | bytes 16252928 | tf_op jit(solution)/shard_map/kcix,tkcyai->tkcayx/dot_general | solution.py:103
  88.3 3.7 %fusion = (bf16[2,1,32,12,16,64]{5,4,3,0,2,1:T(8,128)(2,1)S(1)}, bf16[2,1,32,12,16,64]{5,4,3,0,2,1:T(8,128)(2,1)S(1)}) fusion(f32[2,1,32,12,32,128]{5,4,3,0,2,1:T(8,128)S(1)} %fusion.6), kind=kLoop, calls=%fused_computation.3 | loop fusion | flops 3145728 | bytes 15728640 | tf_op jit(solution)/shard_map/convert.6
  93.3 2.1 fusion.17
  95.4 1.6 collective-permute-start
  97.0 1.7 fusion.14
  99.3 2.0 pad_maximum_fusion.2
  102.0 2.1 %pad_maximum_fusion = bf16[1,384,16,128]{3,2,1,0:T(8,128)(2,1)} fusion(bf16[1,384,16,64]{3,2,1,0:T(8,128)(2,1)S(1)} %get-tuple-element.14, bf16[1,384,16,64]{3,2,1,0:T(8,128)(2,1)S(1)} %get-tuple-element.13), kind=kLoop, calls=%fused_computation.47 | loop fusion | flops 3145728 | bytes 3145728 | tf_op jit(solution)/shard_map/concatenate | solution.py:27
  104.1 42.1 %all-reduce.3.cloned.1.call-done = (bf16[1,384,1536]{2,1,0:T(8,128)(2,1)}, bf16[1,384,1536]{2,1,0:T(8,128)(2,1)}) async-done(((bf16[1,384,1536]{2,1,0:T(8,128)(2,1)}, bf16[1,384,1536]{2,1,0:T(8,128)(2,1)}), (bf16[1,384,1536]{2,1,0:T(8,128)(2,1)}, bf16[1,384,1536]{2,1,0:T(8,128)(2,1)})) %all-reduce.3.cloned.1.call-update) | async-done | bytes 2359312 | tf_op jit(solution)/shard_map/psum | solution.py:17
  146.2 1.4 constant_dynamic-update-slice_fusion.1
  148.0 1.3 fusion.20
  149.3 0.9 copy-done.4
  150.2 2.5 %fusion.11 = bf16[1,384,2048]{1,2,0:T(8,128)(2,1)} fusion(f32[2048,384]{1,0:T(8,128)S(1)} %fusion.20, bf16[48,8,16,128]{3,2,1,0:T(8,128)(2,1)S(1)} %bitcast.157, bf16[2,384,1536]{2,1,0:T(8,128)(2,1)S(1)} %constant_dynamic-update-slice_fusion, s32[]{:T(128)S(6)} %select_n.104, s32[]{:T(128)S(6)} %select_n.98), kind=kOutput, calls=%fused_computation.23 | convolution fusion | flops 605552640 | bytes 6586376 | tf_op jit(solution)/shard_map/ab,kbx->kax/dot_general | solution.py:37
  152.7 2.6 %copy.55 = bf16[1,384,2048]{2,1,0:T(8,128)(2,1)} copy(bf16[1,384,2048]{1,2,0:T(8,128)(2,1)} %fusion.11) | data formatting | bytes 3145728 | tf_op jit(solution)/shard_map/convert_element_type | solution.py:128
  155.3 3.7 %convert_element_type.101 = bf16[6144,128]{1,0:T(8,128)(2,1)} reshape(bf16[1,384,2048]{2,1,0:T(8,128)(2,1)} %copy.55) | data formatting | bytes 3145728 | tf_op jit(solution)/shard_map/convert_element_type | solution.py:128
  159.1 2.3 %fusion.30 = f32[2048,384]{1,0:T(8,128)S(1)} fusion(bf16[48,8,16,128]{3,2,1,0:T(8,128)(2,1)S(1)} %bitcast.144, bf16[2,384,1536]{2,1,0:T(8,128)(2,1)} %copy-done.5, s32[]{:T(128)S(6)} %select_n.94, s32[]{:T(128)S(6)} %select_n.96), kind=kOutput, calls=%fused_computation.41 | convolution fusion | flops 603979776 | bytes 5013512 | tf_op jit(solution)/shard_map/ab,kbx->kax/dot_general | solution.py:36
  161.3 2.6 %slice_negate_fusion.1 = (bf16[1,384,16,64]{3,2,1,0:T(8,128)(2,1)S(1)}, bf16[1,384,16,64]{3,2,1,0:T(8,128)(2,1)S(1)}) fusion(bf16[1,384,16,128]{3,2,1,0:T(8,128)(2,1)} %bitcast.31), kind=kLoop, calls=%fused_computation.45 | loop fusion | flops 393216 | bytes 3145728 | tf_op jit(solution)/shard_map/neg | solution.py:27
  163.9 0.9 pad_maximum_fusion.1
  164.8 2.2 %fusion.23 = f32[2048,384]{1,0:T(8,128)S(1)} fusion(bf16[48,8,16,128]{3,2,1,0:T(8,128)(2,1)S(1)} %bitcast.154, bf16[2,384,1536]{2,1,0:T(8,128)(2,1)} %copy-done.5, s32[]{:T(128)S(6)} %select_n.94, s32[]{:T(128)S(6)} %select_n.103), kind=kOutput, calls=%fused_computation.34 | convolution fusion | flops 603979776 | bytes 5013512 | tf_op jit(solution)/shard_map/ab,kbx->kax/dot_general | solution.py:37
  167.0 2.8 %convolution_add_fusion = f32[2048,384]{1,0:T(8,128)S(1)} fusion(f32[2048,384]{1,0:T(8,128)S(1)} %fusion.23, bf16[48,8,16,128]{3,2,1,0:T(8,128)(2,1)} %bitcast.70, bf16[2,384,1536]{2,1,0:T(8,128)(2,1)} %copy-done.5, s32[]{:T(128)S(6)} %select_n.94, s32[]{:T(128)S(6)} %select_n.101), kind=kOutput, calls=%fused_computation.17 | convolution fusion | flops 604766208 | bytes 8159240 | tf_op jit(solution)/shard_map/ab,kbx->kax/dot_general | solution.py:36
  169.8 1.3 convert_bitcast_fusion
  171.8 3.6 %fusion.10 = bf16[1,384,2048]{1,2,0:T(8,128)(2,1)} fusion(f32[2048,384]{1,0:T(8,128)S(1)} %convolution_add_fusion, f32[2048,384]{1,0:T(8,128)S(1)} %fusion.30, bf16[48,8,16,128]{3,2,1,0:T(8,128)(2,1)S(1)} %bitcast.156, bf16[2,384,1536]{2,1,0:T(8,128)(2,1)} %copy-done.5, s32[]{:T(128)S(6)} %select_n.94, s32[]{:T(128)S(6)} %select_n.98), kind=kOutput, calls=%fused_computation.22 | convolution fusion | flops 606339072 | bytes 9732104 | tf_op jit(solution)/shard_map/ab,kbx->kax/dot_general | solution.py:37
  175.4 2.7 %copy.54 = bf16[1,384,2048]{2,1,0:T(8,128)(2,1)} copy(bf16[1,384,2048]{1,2,0:T(8,128)(2,1)} %fusion.10) | data formatting | bytes 3145728 | tf_op jit(solution)/shard_map/convert_element_type | solution.py:125
  178.1 3.7 %convert_element_type.97 = bf16[6144,128]{1,0:T(8,128)(2,1)} reshape(bf16[1,384,2048]{2,1,0:T(8,128)(2,1)} %copy.54) | data formatting | bytes 3145728 | tf_op jit(solution)/shard_map/convert_element_type | solution.py:125
  181.8 2.6 %copy.56 = bf16[1,384,2048]{2,1,0:T(8,128)(2,1)} copy(bf16[1,384,2048]{1,2,0:T(8,128)(2,1)} %convert_bitcast_fusion) | data formatting | bytes 3145728 | tf_op jit(solution)/shard_map/convert_element_type | solution.py:131
  184.4 3.7 %convert_element_type.105 = bf16[6144,128]{1,0:T(8,128)(2,1)} reshape(bf16[1,384,2048]{2,1,0:T(8,128)(2,1)} %copy.56) | data formatting | bytes 3145728 | tf_op jit(solution)/shard_map/convert_element_type | solution.py:131
  188.2 2.1 %fusion.64 = f32[128,128]{1,0:T(8,128)S(1)} fusion(bf16[6144,128]{1,0:T(8,128)(2,1)S(1)} %bitcast.145, bf16[6144,128]{1,0:T(8,128)(2,1)} %convert_element_type.97), kind=kOutput, calls=%fused_computation.104 | convolution fusion | flops 201326592 | bytes 3211264 | tf_op jit(solution)/shard_map/kxm,kxn->kmn/dot_general | solution.py:48
  191.0 0.8 copy-done.2
  192.5 0.7 fusion.54
  193.2 9.4 %reduce-scatter.2.cloned.1.call-done = bf16[1,32,128]{2,1,0:T(8,128)(2,1)} async-done(((bf16[1,64,128]{2,1,0:T(8,128)(2,1)}), bf16[1,32,128]{2,1,0:T(8,128)(2,1)}) %reduce-scatter.2.cloned.1.call-update) | async-done | bytes 8208 | tf_op jit(solution)/shard_map/reduce_scatter | solution.py:139
  202.6 1.3 convert_element_type.107
  (55 shorter events, 10.6 us)
Async XLA Ops:
  9.7 11.6 %copy-start.9 = (s32[2,16]{1,0:T(2,128)S(1)}, s32[2,16]{1,0:T(2,128)}, u32[]{:S(2)}) copy-start(s32[2,16]{1,0:T(2,128)} %param.10) | copy-start | bytes 388
  9.8 11.7 %copy-start.8 = (s32[2]{0:T(128)S(1)}, s32[2]{0:T(128)}, u32[]{:S(2)}) copy-start(s32[2]{0:T(128)} %param.11) | copy-start | bytes 28
  13.9 17.4 %all-to-all-start = ((bf16[16,2,4096]{2,1,0:T(2,128)(2,1)}), bf16[16,2,4096]{2,1,0:T(2,128)(2,1)S(1)}, u32[]{:S(2)}, u32[]{:S(2)}) async-start(bf16[16,2,4096]{2,1,0:T(2,128)(2,1)} %reshape.297), calls=%async_computation | async-start | bytes 524288 | tf_op jit(solution)/shard_map/all_to_all | solution.py:76
  32.3 4.6 %copy-start.7 = (bf16[1,384,1536]{2,1,0:T(8,128)(2,1)S(1)}, bf16[1,384,1536]{2,1,0:T(8,128)(2,1)}, u32[]{:S(2)}) copy-start(bf16[1,384,1536]{2,1,0:T(8,128)(2,1)} %param.9) | copy-start | bytes 3538948
  33.3 13.5 %all-to-all-start.1 = ((bf16[16,64,128]{2,1,0:T(8,128)(2,1)}), bf16[16,64,128]{2,1,0:T(8,128)(2,1)S(1)}, u32[]{:S(2)}, u32[]{:S(2)}) async-start(bf16[16,64,128]{2,1,0:T(8,128)(2,1)} %get-tuple-element.21), calls=%async_computation.1 | async-start | bytes 524288 | tf_op jit(solution)/shard_map/all_to_all | solution.py:80
  36.8 109.4 %all-reduce.3.cloned.1.call-start = ((), (), s32[]{:S(2)}) async-start(), calls=%async_computation.5 | async-start | bytes 4718592 | tf_op jit(solution)/shard_map/psum | solution.py:17
  38.5 0.7 copy-start.10
  38.5 12.2 %copy-start = (bf16[1,4096,128]{2,1,0:T(8,128)(2,1)S(1)}, bf16[1,4096,128]{2,1,0:T(8,128)(2,1)}, u32[]{:S(2)}) copy-start(bf16[1,4096,128]{2,1,0:T(8,128)(2,1)} %param.6) | copy-start | bytes 3145732
  46.8 16.4 %all-to-all-start.2 = ((bf16[16,64,128]{2,1,0:T(8,128)(2,1)}), bf16[16,64,128]{2,1,0:T(8,128)(2,1)S(1)}, u32[]{:S(2)}, u32[]{:S(2)}) async-start(bf16[16,64,128]{2,1,0:T(8,128)(2,1)} %get-tuple-element.22), calls=%async_computation.2 | async-start | bytes 524288 | tf_op jit(solution)/shard_map/all_to_all | solution.py:80
  50.3 152.2 %reduce-scatter.2.cloned.1.call-start = ((), (), s32[]{:S(2)}) async-start(), calls=%async_computation.4 | async-start | bytes 24576 | tf_op jit(solution)/shard_map/reduce_scatter | solution.py:139
  95.4 65.9 %collective-permute-start = (bf16[1,1,384,16,128]{4,3,2,1,0:T(8,128)(2,1)}, bf16[1,1,384,16,128]{4,3,2,1,0:T(8,128)(2,1)}, u32[]{:S(2)}, u32[]{:S(2)}) collective-permute-start(bf16[1,1,384,16,128]{4,3,2,1,0:T(8,128)(2,1)} %fusion.17), channel_id=1, source_target_pairs={{0,1},{1,0},{2,3},{3,2},{4,5},{5,4},{6,7},{7,6},{8,9},{9,8},{10,11... | collective-permute-start | bytes 4718600 | tf_op jit(solution)/shard_map/ppermute | solution.py:23
  146.2 1.6 copy-start.6
  147.9 1.4 copy-start.5
  147.9 2.3 %copy-start.4 = (bf16[1,384,16,128]{3,2,1,0:T(8,128)(2,1)S(1)}, bf16[1,384,16,128]{3,2,1,0:T(8,128)(2,1)}, u32[]{:S(2)}) copy-start(bf16[1,384,16,128]{3,2,1,0:T(8,128)(2,1)} %pad_maximum_fusion.2) | copy-start | bytes 4718596
  169.8 2.0 copy-start.1
  188.2 2.1 %copy-start.3 = (bf16[6144,128]{1,0:T(8,128)(2,1)S(1)}, bf16[6144,128]{1,0:T(8,128)(2,1)}, u32[]{:S(2)}) copy-start(bf16[6144,128]{1,0:T(8,128)(2,1)} %convert_element_type.105) | copy-start | bytes 4718596
  190.3 1.4 copy-start.2
Sparse Core Ops, SparseCore 0:
  41.2 104.9 all-reduce.2
  193.3 9.2 reduce-scatter.1
where the time goes:
time: 212 us; the launch traced here: 211 us
  waiting for transfers between devices  78.2 us (37%)
  local copies, waits for them, and re-layouts  47.6 us (22%)
  matrix products  28.1 us (13%)
  other arithmetic  25.5 us (12%)
  starting transfers between devices  16.3 us (8%)
  between operations  15.1 us (7%)
    psum x1, waiting for transfers between devices, from_root(): return lax.psum(block, axis)  42.1 us
    all_to_all x2, waiting for transfers between devices, local(): lax.all_to_all(permuted[momentum_transfer], 'ka', split_axis=0, concat_ax...  18.6 us
    reduce_scatter x1, waiting for transfers between devices, local(): lax.psum_scatter(local_sigma.astype(jnp.bfloat16), 'aux', scatter_dimensi...  9.4 us
    another operation x3, local copies, waits for them, and re-layouts  8.42 us
    dot_general x3, matrix products, apply_block(): jnp.einsum('ab,kbx->kax', imag_cols, turned, preferred_element_type=jnp.f...  8.36 us
    all_to_all x1, waiting for transfers between devices, local(): lax.all_to_all(packed, 'ka', split_axis=1, concat_axis=0, tiled=True)  8.01 us
    all_to_all x1, starting transfers between devices, local(): lax.all_to_all(packed, 'ka', split_axis=1, concat_axis=0, tiled=True)  7.41 us
    all_to_all x2, starting transfers between devices, local(): lax.all_to_all(permuted[momentum_transfer], 'ka', split_axis=0, concat_ax...  7.06 us
  transfers between devices with their start and end apart: 6, of which 5 were waited for; matrix products, arithmetic and copies ran while one was open for 27% of the time, Pallas kernels for 0%

commit v1 on v0

--- a/solution.py
+++ b/solution.py
@@ -14,7 +14,7 @@
 
 def from_root(block, axis, source):
     block = jnp.where(lax.axis_index(axis) == source, block, jnp.zeros_like(block))
-    return lax.psum(block, axis)
+    return jnp.sum(lax.all_gather(block, axis), axis=0)
 
 
 def from_partner(value, axis, distance):

time: 212 us -> 299 us (1.41)
  waiting for transfers between devices: 78.2 us -> 145 us
  other arithmetic: 25.5 us -> 51 us
    all_gather x0 -> x2, waiting for transfers between devices: none -> 67.7 us  [from_root(): return jnp.sum(lax.all_gather(block, axis), axis=0)]
    psum x1 -> x0, waiting for transfers between devices: 42.1 us -> none  [from_root(): return lax.psum(block, axis)]
    ppermute x1, waiting for transfers between devices: 0.01 us -> 24.7 us  [from_partner(): return lax.ppermute(value, axis, pairs)]
    reduce_sum x0 -> x2, other arithmetic: none -> 22.2 us  [from_root(): return jnp.sum(lax.all_gather(block, axis), axis=0)]
    all_to_all x2, waiting for transfers between devices: 18.6 us -> 27.4 us  [local(): lax.all_to_all(permuted[momentum_transfer], 'ka', split_axis=0, concat_ax...]
    all_to_all x1, waiting for transfers between devices: 8.01 us -> 14.5 us  [local(): lax.all_to_all(packed, 'ka', split_axis=1, concat_axis=0, tiled=True)]
    unnamed x29 -> x42, local copies, waits for them, and re-layouts: 6.87 us -> 7.49 us
    another operation x4 -> x3, local copies, waits for them, and re-layouts: 8.49 us -> 8.19 us
  transfers between devices with their start and end apart: 6 -> 7, of which waited for: 5 -> 6; matrix products, arithmetic and copies ran while one was open for 27% -> 22% of each run, Pallas kernels for 0% -> 0%
where the time goes in v1:
time: 299 us; the launch traced here: 298 us
  waiting for transfers between devices  145 us (48%)
  other arithmetic  51 us (17%)
  local copies, waits for them, and re-layouts  44.9 us (15%)
  matrix products  25.9 us (9%)
  starting transfers between devices  16.2 us (5%)
  between operations  14.7 us (5%)
    all_gather x2, waiting for transfers between devices, from_root(): return jnp.sum(lax.all_gather(block, axis), axis=0)  67.7 us
    all_to_all x2, waiting for transfers between devices, local(): lax.all_to_all(permuted[momentum_transfer], 'ka', split_axis=0, concat_ax...  27.4 us
    ppermute x1, waiting for transfers between devices, from_partner(): return lax.ppermute(value, axis, pairs)  24.7 us
    reduce_sum x2, other arithmetic, from_root(): return jnp.sum(lax.all_gather(block, axis), axis=0)  22.2 us
    all_to_all x1, waiting for transfers between devices, local(): lax.all_to_all(packed, 'ka', split_axis=1, concat_axis=0, tiled=True)  14.5 us
    reduce_scatter x1, waiting for transfers between devices, local(): lax.psum_scatter(local_sigma.astype(jnp.bfloat16), 'aux', scatter_dimensi...  9.93 us
    another operation x3, local copies, waits for them, and re-layouts  8.19 us
    unnamed x42, local copies, waits for them, and re-layouts  7.49 us
  transfers between devices with their start and end apart: 7, of which 6 were waited for; matrix products, arithmetic and copies ran while one was open for 22% of the time, Pallas kernels for 0%

profile of v1, /device:TPU:0, one launch (start us, length us, event | category | flops | bytes accessed | tf_op | source)
XLA Modules:
  0.0 297.7 jit_solution(99819223803620270)
XLA Ops:
  6.5 1.3 fusion.75
  9.1 2.9 broadcast_select_fusion
  15.9 2.2 reduce.2
  18.1 0.8 reshape.289
  18.9 7.4 %all-to-all-start = ((bf16[16,2,4096]{2,1,0:T(2,128)(2,1)}), bf16[16,2,4096]{2,1,0:T(2,128)(2,1)S(1)}, u32[]{:S(2)}, u32[]{:S(2)}) async-start(bf16[16,2,4096]{2,1,0:T(2,128)(2,1)} %reshape.289), calls=%async_computation | async-start | bytes 524288 | tf_op jit(solution)/shard_map/all_to_all | solution.py:76
  26.4 14.5 %all-to-all-done = bf16[16,2,4096]{2,1,0:T(2,128)(2,1)S(1)} async-done(((bf16[16,2,4096]{2,1,0:T(2,128)(2,1)}), bf16[16,2,4096]{2,1,0:T(2,128)(2,1)S(1)}, u32[]{:S(2)}, u32[]{:S(2)}) %all-to-all-start) | async-done | bytes 262176 | tf_op jit(solution)/shard_map/all_to_all | solution.py:76
  42.0 0.8 slice_bitcast_fusion.1
  42.9 3.5 %all-to-all-start.2 = ((bf16[16,64,128]{2,1,0:T(8,128)(2,1)}), bf16[16,64,128]{2,1,0:T(8,128)(2,1)S(1)}, u32[]{:S(2)}, u32[]{:S(2)}) async-start(bf16[16,64,128]{2,1,0:T(8,128)(2,1)} %get-tuple-element.20), calls=%async_computation.2 | async-start | bytes 524288 | tf_op jit(solution)/shard_map/all_to_all | solution.py:80
  46.6 14.5 %all-to-all-done.2 = bf16[16,64,128]{2,1,0:T(8,128)(2,1)S(1)} async-done(((bf16[16,64,128]{2,1,0:T(8,128)(2,1)}), bf16[16,64,128]{2,1,0:T(8,128)(2,1)S(1)}, u32[]{:S(2)}, u32[]{:S(2)}) %all-to-all-start.2) | async-done | bytes 262176 | tf_op jit(solution)/shard_map/all_to_all | solution.py:80
  61.0 3.5 %all-to-all-start.1 = ((bf16[16,64,128]{2,1,0:T(8,128)(2,1)}), bf16[16,64,128]{2,1,0:T(8,128)(2,1)S(1)}, u32[]{:S(2)}, u32[]{:S(2)}) async-start(bf16[16,64,128]{2,1,0:T(8,128)(2,1)} %get-tuple-element.19), calls=%async_computation.1 | async-start | bytes 524288 | tf_op jit(solution)/shard_map/all_to_all | solution.py:80
  65.0 0.8 constant_dynamic-slice_fusion
  66.3 12.9 %all-to-all-done.1 = bf16[16,64,128]{2,1,0:T(8,128)(2,1)S(1)} async-done(((bf16[16,64,128]{2,1,0:T(8,128)(2,1)}), bf16[16,64,128]{2,1,0:T(8,128)(2,1)S(1)}, u32[]{:S(2)}, u32[]{:S(2)}) %all-to-all-start.1) | async-done | bytes 262176 | tf_op jit(solution)/shard_map/all_to_all | solution.py:80
  79.2 1.4 stack.18
  80.6 1.7 maximum_bitcast_fusion
  82.3 2.1 gather_fusion.1
  84.4 2.7 copy.46
  87.1 5.0 %fusion.9 = bf16[2,1,32,32,768]{4,3,0,2,1:T(8,128)(2,1)S(1)} fusion(bf16[32,2,64,768]{3,2,1,0:T(8,128)(2,1)} %param.7, bf16[32,2,2,64,32]{3,4,2,1,0:T(8,128)(2,1)} %bitcast.170, pred[32,2]{1,0:T(8,128)(4,1)S(1)} %copy.40), kind=kOutput, calls=%fused_computation.24 | convolution fusion | flops 404488192 | bytes 9961536 | tf_op jit(solution)/shard_map/tkcjoy,cjox->tkcyx/dot_general | solution.py:97
  92.1 7.1 %reshape.288 = bf16[2,32,32,12,64]{4,3,2,0,1:T(8,128)(2,1)} reshape(bf16[2,1,32,32,768]{4,3,0,2,1:T(8,128)(2,1)S(1)} %fusion.9) | data formatting | bytes 6291456 | tf_op jit(solution)/shard_map/reshape.12
  99.2 5.3 %fusion.6 = f32[2,1,32,12,32,128]{5,4,3,0,2,1:T(8,128)S(1)} fusion(bf16[32,64,128,1,1]{2,1,4,3,0:T(8,128)(2,1)} %bitcast.176, bf16[2,32,32,12,64]{4,3,2,0,1:T(8,128)(2,1)} %reshape.288), kind=kOutput, calls=%fused_computation.11 | convolution fusion | flops 402653184 | bytes 16252928 | tf_op jit(solution)/shard_map/kcix,tkcyai->tkcayx/dot_general | solution.py:103
  104.5 3.7 %fusion = (bf16[2,1,32,12,16,64]{5,4,3,0,2,1:T(8,128)(2,1)S(1)}, bf16[2,1,32,12,16,64]{5,4,3,0,2,1:T(8,128)(2,1)S(1)}) fusion(f32[2,1,32,12,32,128]{5,4,3,0,2,1:T(8,128)S(1)} %fusion.6), kind=kLoop, calls=%fused_computation.3 | loop fusion | flops 3145728 | bytes 15728640 | tf_op jit(solution)/shard_map/convert.8
  109.4 1.1 copy-done.8
  110.5 2.0 fusion.17
  112.5 1.5 collective-permute-start
  114.0 4.6 %fusion.14 = (bf16[1,1,384,16,128]{4,3,2,0,1:T(8,128)(2,1)S(1)}, bf16[1,1,384,16,128]{4,3,2,0,1:T(8,128)(2,1)S(1)}) fusion(s32[]{:T(128)S(6)} %select_n.93, bf16[2,1,384,16,64]{4,3,2,0,1:T(8,128)(2,1)} %bitcast.167, bf16[2,1,384,16,64]{4,3,2,0,1:T(8,128)(2,1)} %bitcast.165, s32[]{:T(128)S(6)} %select_n.83), kind=kLoop, calls=%fused_computation.37 | loop fusion | flops 6291456 | bytes 6291464 | tf_op jit(solution)/shard_map/concatenate | solution.py:112
  119.3 2.0 pad_maximum_fusion
  122.0 2.0 pad_maximum_fusion.2
  124.0 24.7 %collective-permute-done = bf16[1,1,384,16,128]{4,3,2,1,0:T(8,128)(2,1)S(1)} collective-permute-done((bf16[1,1,384,16,128]{4,3,2,1,0:T(8,128)(2,1)}, bf16[1,1,384,16,128]{4,3,2,1,0:T(8,128)(2,1)S(1)}, u32[]{:S(2)}, u32[]{:S(2)}) %collective-permute-start) | collective-permute-done | bytes 1572896 | tf_op jit(solution)/shard_map/ppermute | solution.py:23
  149.9 2.0 pad_maximum_fusion.1
  151.9 10.6 %reduce_sum.25 = bf16[384,1536]{1,0:T(8,128)(2,1)S(1)} reduce(bf16[16,384,1536]{2,1,0:T(8,128)(2,1)} %all-gather.5.cloned.1.call-done, bf16[]{:T(256)} %constant.170.clone.1), dimensions={0}, to_apply=%region_1.2 | reduce | flops 8847360 | bytes 20054018 | tf_op jit(solution)/shard_map/reduce_sum | solution.py:17
  162.5 67.7 %all-gather.3.cloned.1.call-done = bf16[16,384,1536]{2,1,0:T(8,128)(2,1)} async-done(((bf16[1,384,1536]{2,1,0:T(8,128)(2,1)}), bf16[16,384,1536]{2,1,0:T(8,128)(2,1)}) %all-gather.3.cloned.1.call-update) | async-done | bytes 18874384 | tf_op jit(solution)/shard_map/all_gather | solution.py:17
  230.2 11.6 %reduce_sum.24 = bf16[384,1536]{1,0:T(8,128)(2,1)} reduce(bf16[16,384,1536]{2,1,0:T(8,128)(2,1)} %all-gather.3.cloned.1.call-done, bf16[]{:T(256)} %constant.170.clone.1), dimensions={0}, to_apply=%region_0.1 | reduce | flops 8847360 | bytes 20054018 | tf_op jit(solution)/shard_map/reduce_sum | solution.py:17
  241.8 2.9 fusion.23
  244.7 1.4 convolution_add_fusion
  246.1 1.6 copy-done.6
  247.8 1.3 convert_bitcast_fusion
  249.1 2.6 copy.56
  251.7 3.8 %convert_element_type.109 = bf16[6144,128]{1,0:T(8,128)(2,1)} reshape(bf16[1,384,2048]{2,1,0:T(8,128)(2,1)} %copy.56) | data formatting | bytes 3145728 | tf_op jit(solution)/shard_map/convert_element_type | solution.py:131
  255.5 2.5 fusion.30
  258.3 2.7 fusion.10
  261.1 2.6 copy.54
  263.6 3.7 %convert_element_type.101 = bf16[6144,128]{1,0:T(8,128)(2,1)} reshape(bf16[1,384,2048]{2,1,0:T(8,128)(2,1)} %copy.54) | data formatting | bytes 3145728 | tf_op jit(solution)/shard_map/convert_element_type | solution.py:125
  267.4 2.1 convolution_bitcast_fusion
  271.3 1.3 fusion.20
  272.7 1.4 fusion.11
  274.2 1.6 copy.55
  275.8 2.7 convert_element_type.105
  280.0 9.9 %reduce-scatter.2.cloned.1.call-done = bf16[1,32,128]{2,1,0:T(8,128)(2,1)} async-done(((bf16[1,64,128]{2,1,0:T(8,128)(2,1)}), bf16[1,32,128]{2,1,0:T(8,128)(2,1)}) %reduce-scatter.2.cloned.1.call-update) | async-done | bytes 8208 | tf_op jit(solution)/shard_map/reduce_scatter | solution.py:139
  289.9 1.3 convert_element_type.111
  (72 shorter events, 13.2 us)
Async XLA Ops:
  6.5 145.3 %all-gather.5.cloned.1.call-start = ((), (), s32[]{:S(2)}) async-start(), calls=%async_computation.5 | async-start | bytes 20054016 | tf_op jit(solution)/shard_map/all_gather | solution.py:17
  12.0 1.2 copy-start.12
  12.0 218.2 %all-gather.3.cloned.1.call-start = ((), (), s32[]{:S(2)}) async-start(), calls=%async_computation.4 | async-start | bytes 20054016 | tf_op jit(solution)/shard_map/all_gather | solution.py:17
  14.7 11.6 %copy-start.16 = (s32[2,16]{1,0:T(2,128)S(1)}, s32[2,16]{1,0:T(2,128)}, u32[]{:S(2)}) copy-start(s32[2,16]{1,0:T(2,128)} %param.10) | copy-start | bytes 388
  18.9 22.1 %all-to-all-start = ((bf16[16,2,4096]{2,1,0:T(2,128)(2,1)}), bf16[16,2,4096]{2,1,0:T(2,128)(2,1)S(1)}, u32[]{:S(2)}, u32[]{:S(2)}) async-start(bf16[16,2,4096]{2,1,0:T(2,128)(2,1)} %reshape.289), calls=%async_computation | async-start | bytes 524288 | tf_op jit(solution)/shard_map/all_to_all | solution.py:76
  41.9 4.5 %copy-start.17 = (s32[32,2]{0,1:T(2,128)S(1)}, s32[32,2]{0,1:T(2,128)}, u32[]{:S(2)}) copy-start(s32[32,2]{0,1:T(2,128)} %param.8) | copy-start | bytes 772
  42.9 18.2 %all-to-all-start.2 = ((bf16[16,64,128]{2,1,0:T(8,128)(2,1)}), bf16[16,64,128]{2,1,0:T(8,128)(2,1)S(1)}, u32[]{:S(2)}, u32[]{:S(2)}) async-start(bf16[16,64,128]{2,1,0:T(8,128)(2,1)} %get-tuple-element.20), calls=%async_computation.2 | async-start | bytes 524288 | tf_op jit(solution)/shard_map/all_to_all | solution.py:80
  61.0 18.2 %all-to-all-start.1 = ((bf16[16,64,128]{2,1,0:T(8,128)(2,1)}), bf16[16,64,128]{2,1,0:T(8,128)(2,1)S(1)}, u32[]{:S(2)}, u32[]{:S(2)}) async-start(bf16[16,64,128]{2,1,0:T(8,128)(2,1)} %get-tuple-element.19), calls=%async_computation.1 | async-start | bytes 524288 | tf_op jit(solution)/shard_map/all_to_all | solution.py:80
  64.6 225.3 %reduce-scatter.2.cloned.1.call-start = ((), (), s32[]{:S(2)}) async-start(), calls=%async_computation.6 | async-start | bytes 24576 | tf_op jit(solution)/shard_map/reduce_scatter | solution.py:139
  108.8 1.7 copy-start.8
  109.3 3.1 %copy-start.9 = (bf16[2,1,32,12,16,64]{5,4,3,2,0,1:T(8,128)(2,1)}, bf16[2,1,32,12,16,64]{5,4,3,2,0,1:T(8,128)(2,1)S(1)}, u32[]{:S(2)}) copy-start(bf16[2,1,32,12,16,64]{5,4,3,2,0,1:T(8,128)(2,1)S(1)} %copy.50) | copy-start | bytes 4718596
  112.5 36.2 %collective-permute-start = (bf16[1,1,384,16,128]{4,3,2,1,0:T(8,128)(2,1)}, bf16[1,1,384,16,128]{4,3,2,1,0:T(8,128)(2,1)S(1)}, u32[]{:S(2)}, u32[]{:S(2)}) collective-permute-start(bf16[1,1,384,16,128]{4,3,2,1,0:T(8,128)(2,1)} %fusion.17), channel_id=1, source_target_pairs={{0,1},{1,0},{2,3},{3,2},{4,5},{5,4},{6,7},{7,6},{8,9},{9,8},{10,11... | collective-permute-start | bytes 4718600 | tf_op jit(solution)/shard_map/ppermute | solution.py:23
  118.6 2.7 copy-start.3
  148.7 1.2 copy-start.10
  241.8 2.9 copy-start
  241.8 2.9 copy-start.11
  246.1 1.6 copy-start.6
  255.5 2.5 copy-start.1
  255.5 2.5 copy-start.7
  255.5 2.8 copy-start.14
  267.4 2.1 copy-start.15
  269.5 1.3 copy-start.2
  269.5 1.8 copy-start.4
  271.3 1.4 copy-start.13
  275.8 2.7 copy-start.5
Sparse Core Ops, SparseCore 0:
  12.1 114.2 all-gather.4
  128.0 102.1 all-gather.2
  280.1 9.7 reduce-scatter.1
